TPU v7x, 512 devices: a whole 4x4x16 slice. The times are simulated.
512 devices in a mesh: rows: 128 (over x, z_lo, y), feat: 4 (over z_hi, core).
Axes of the slice: x: 4, y: 4, z: 16 (z_hi: 2, z_lo: 8; z = z_hi * 8 + z_lo), core: 2. Of those that a mesh axis runs over, the one named last changes fastest.
Arguments:
- features: bfloat16 [32768, 512], P('rows', 'feat'), may hold values from -6 to 6
- weight: bfloat16 [512, 512], P(None, 'feat'), may hold values from -0.25 to 0.25
- block_values: bfloat16 [256, 8, 128, 128], P('rows', 'feat'), may hold values from -0.25 to 0.25
- columns: int32 [256, 8], P('rows'), may hold values from 0 to 255, as said below
- counts: int32 [256], P('rows'), may hold values from 2 to 8, as said below
- cotangent: bfloat16 [32768, 512], P('rows', 'feat'), may hold values from -6 to 6
Outputs:
- hidden: bfloat16 [32768, 512], P('rows', 'feat')
- grad_features: bfloat16 [32768, 512], P('rows', 'feat')
- grad_weight: float32 [512, 512], P(None, 'feat')
Inputs may be any that keep to these rules, and one draw needn't show every extreme that they name: `columns`: the 8 column blocks of a row block are distinct and lie on the devices within 4 indices of the row block's own index along rows, counted around the axis (the device of block c is c // 2). Slots 0 to counts[g] - 1 of row block g are live, the others are ignored; some row block has exactly 8 live slots.
All inputs are finite; a program needn't handle non-finite values.
Results may differ from a plain program's by a relative error of at most 0.0067.
Values may be sent and summed in bfloat16 or wider, within the bound.
No kernel may reach another device: no remote copies, remote signals or barrier semaphores. Data moves between devices by JAX's collectives and lax.ppermute only.
A program may use at most 64 MiB of HBM per device.

v0:
```python
import jax
import jax.numpy as jnp
from jax import lax
from jax.experimental import pallas as pl
from jax.experimental.pallas import tpu as pltpu
from jax.sharding import PartitionSpec as P


X, ZL, Y = 4, 8, 4
R = X * ZL * Y
FB = 128
RB = 2
REACH = 4
STEP_Y = [[(r, r // 4 * 4 + (r + k) % 4) for r in range(R)] for k in range(4)]
SWAP_A = [(r, (r + 4) % R if (r // 4) % 2 == 0 else (r - 4) % R) for r in range(R)]
SWAP_B = [(r, (r - 4) % R if (r // 4) % 2 == 0 else (r + 4) % R) for r in range(R)]
CROSS = [(f, f ^ 2) for f in range(4)]
SIBLING = [(f, f ^ 1) for f in range(4)]
FLIPS = (0, 2, 1, 3)
F32 = jnp.float32
BF16 = jnp.bfloat16


def window_place(col, r, sign):
    y = r & 3
    off = ((col >> 1) - r + REACH + R) & (R - 1)
    t = y + off
    s = t & 3
    dq = (t >> 2) - 1
    k = (sign * (s - y)) & 3
    piece = jnp.where(dq == 0, k * 2, jnp.where((dq == 1) & (k == 0), 8, k * 2 + 1))
    return jnp.clip(piece * 2 + (col & 1), 0, 17)


def slot_of(p, j, f):
    return (f ^ FLIPS[p]) * 2 + j


def panel_tile(refs, p, g, j):
    own, cross, pair = refs
    ref, start = ((own, 0), (cross, 0), (pair, 0), (pair, 4 * FB))[p]
    base = start + (g * 2 + j) * FB
    return ref[base : base + FB, :]


def gather_kernel(ids, columns, counts, own, cross, pair, near, before, win1, win2, win3, after, agg, win):
    r, f = ids[0], ids[1]
    for start, ref in ((0, near), (2, before), (4, win1), (8, win2), (12, win3), (16, after)):
        win[start : start + ref.shape[0]] = ref[...]
    for g in range(RB):
        total = jnp.zeros((FB, FB), F32)
        for p in range(4):
            for j in range(2):
                slot = slot_of(p, j, f)
                place = window_place(columns[g, slot], r, -1)
                tile = panel_tile((own, cross, pair), p, g, j)
                tile = jnp.where(counts[g] > slot, tile, jnp.zeros_like(tile))
                block = win[place]
                total = total + jnp.dot(tile, block, preferred_element_type=F32)
        agg[g * FB : (g + 1) * FB, :] = total.astype(BF16)


def layer_kernel(ids, own, cross, pair, agg, hidden, terms, grad):
    f = ids[1]
    k0 = 0.7978845608028654
    wide = jnp.concatenate([agg[k] for k in range(4)], axis=1)
    grad_agg = jnp.zeros((RB * FB, FB), F32)
    for p in range(4):
        ref, start = ((own, 0), (cross, 0), (pair, 0), (pair, 6 * FB))[p]
        weight = ref[start + 2 * FB : start + 6 * FB, :]
        cot = ref[start : start + 2 * FB, :].astype(F32)
        v = jnp.dot(wide, weight, preferred_element_type=F32)
        v2 = v * v
        t = jnp.tanh(k0 * (v + 0.044715 * (v * v2)))
        half = 0.5 * (1.0 + t)
        if p == 0:
            hidden[...] = (v * half).astype(BF16)
        slope = half + 0.5 * v * (1.0 - t * t) * (k0 * (1.0 + 3 * 0.044715 * v2))
        grad_pre = (cot * slope).astype(BF16)
        if p == 0:
            terms[...] = lax.dot_general(
                wide, grad_pre, (((0,), (0,)), ((), ())), preferred_element_type=F32
            ).astype(BF16)
        rows = ref[pl.ds(pl.multiple_of(start + 2 * FB + f * FB, FB), FB), :]
        grad_agg = grad_agg + lax.dot_general(
            grad_pre, rows, (((1,), (1,)), ((), ())), preferred_element_type=F32
        )
    grad[...] = grad_agg.astype(BF16)


def spread_kernel(ids, columns, counts, own, cross, pair, grad, mine, send1, send2, send3, wnd):
    r, f = ids[0], ids[1]
    for b in range(18):
        wnd[b] = jnp.zeros((FB, FB), F32)
    for g in range(RB):
        part = grad[g * FB : (g + 1) * FB, :]
        for p in range(4):
            for j in range(2):
                slot = slot_of(p, j, f)
                place = window_place(columns[g, slot], r, 1)
                tile = panel_tile((own, cross, pair), p, g, j)
                tile = jnp.where(counts[g] > slot, tile, jnp.zeros_like(tile))
                product = lax.dot_general(
                    tile, part, (((0,), (0,)), ((), ())), preferred_element_type=F32
                )
                wnd[place] = wnd[place] + product
    for k, ref in ((1, send1), (2, send2), (3, send3)):
        for b in range(4):
            ref[b] = wnd[k * 4 + b].astype(BF16)
    for b in range(4):
        mine[b] = wnd[b]
    for b in range(2):
        mine[4 + b] = wnd[16 + b]


def call(kernel, out_shape, scratch, scalars, *args):
    smem = pl.BlockSpec(memory_space=pltpu.SMEM)
    vmem = pl.BlockSpec(memory_space=pltpu.VMEM)
    return pl.pallas_call(
        kernel,
        out_shape=out_shape,
        in_specs=[smem] * len(scalars) + [vmem] * len(args),
        out_specs=jax.tree.map(lambda _: vmem, out_shape),
        scratch_shapes=scratch,
    )(*scalars, *args)


def blocks(value):
    return value.reshape(-1, FB, FB)


def on_device(features, weight, block_values, columns, counts, cotangent):
    r = lax.axis_index("rows")
    f = lax.axis_index("feat")
    y = r & 3
    even = ((r >> 2) & 1) == 0
    ids = jnp.stack([r, f]).astype(jnp.int32)
    rows = features.shape[0]

    from_b = lax.ppermute(features, "rows", SWAP_B)
    from_a = lax.ppermute(features, "rows", SWAP_A)
    own_p = block_values.reshape(4 * FB, FB)
    cross_p = lax.ppermute(own_p, "feat", CROSS)
    own_w = jnp.concatenate([cotangent, weight], axis=0)
    cross_w = lax.ppermute(own_w, "feat", CROSS)
    nxt = jnp.where(even, from_a, from_b)
    prv = jnp.where(even, from_b, from_a)
    arrived = []
    for k in range(1, 4):
        extra = jnp.where(y < 4 - k, nxt, prv)
        arrived.append(lax.ppermute(jnp.stack([features, extra]), "rows", STEP_Y[k]))
    cross_p, *arrived = lax.optimization_barrier((cross_p, *arrived))
    pair_p = lax.ppermute(jnp.concatenate([own_p, cross_p], axis=0), "feat", SIBLING)
    agg = call(
        gather_kernel,
        jax.ShapeDtypeStruct((rows, FB), BF16),
        [pltpu.VMEM((18, FB, FB), BF16)],
        (ids, columns, counts),
        own_p, cross_p, pair_p, blocks(features), blocks(prv), *map(blocks, arrived), blocks(nxt),
    )
    cross_w, agg = lax.optimization_barrier((cross_w, agg))
    pair_w = lax.ppermute(jnp.concatenate([own_w, cross_w], axis=0), "feat", SIBLING)
    agg_full = lax.all_gather(agg, "feat", axis=0, tiled=False)
    hidden, terms, grad = call(
        layer_kernel,
        (
            jax.ShapeDtypeStruct((rows, FB), BF16),
            jax.ShapeDtypeStruct((4 * FB, FB), BF16),
            jax.ShapeDtypeStruct((rows, FB), BF16),
        ),
        [],
        (ids,),
        own_w, cross_w, pair_w, agg_full,
    )
    parts = lax.all_to_all(terms.reshape(R, 4, FB), "rows", 0, 0, tiled=True)
    mine, *sends = call(
        spread_kernel,
        (
            jax.ShapeDtypeStruct((6, FB, FB), F32),
            jax.ShapeDtypeStruct((4, FB, FB), BF16),
            jax.ShapeDtypeStruct((4, FB, FB), BF16),
            jax.ShapeDtypeStruct((4, FB, FB), BF16),
        ),
        [pltpu.VMEM((18, FB, FB), F32)],
        (ids, columns, counts),
        own_p, cross_p, pair_p, grad,
    )
    got = []
    for k in range(1, 4):
        got.append(lax.ppermute(sends[k - 1].reshape(2, rows, FB), "rows", STEP_Y[k]).astype(F32))
    here, to_prv, to_nxt = mine.reshape(3, rows, FB)
    for k in range(1, 4):
        here = here + got[k - 1][0]
        to_prv = to_prv + jnp.where(y >= k, got[k - 1][1], 0.0)
        to_nxt = to_nxt + jnp.where(y < k, got[k - 1][1], 0.0)
    to_prv, to_nxt = to_prv.astype(BF16), to_nxt.astype(BF16)
    back_b = lax.ppermute(jnp.where(even, to_prv, to_nxt), "rows", SWAP_B)
    back_a = lax.ppermute(jnp.where(even, to_nxt, to_prv), "rows", SWAP_A)
    grad_features = (here + back_a.astype(F32) + back_b.astype(F32)).astype(BF16)

    total = (parts.astype(F32).sum(0) * float(rows * R) ** (-0.5)).astype(BF16)
    grad_weight = lax.all_to_all(
        jnp.broadcast_to(total[None], (R, 4, FB)), "rows", 0, 0, tiled=True
    )
    return hidden, grad_features, grad_weight.reshape(4 * FB, FB).astype(F32)


def solution(mesh):
    in_specs = (
        P("rows", "feat"),
        P(None, "feat"),
        P("rows", "feat", None, None),
        P("rows", None),
        P("rows"),
        P("rows", "feat"),
    )
    out_specs = (P("rows", "feat"), P("rows", "feat"), P(None, "feat"))
    return jax.shard_map(
        on_device, mesh=mesh, in_specs=in_specs, out_specs=out_specs, check_vma=False
    )
```

profile of v0, /device:TPU:8, one launch (start us, length us, event | category | flops | bytes accessed | tf_op | source)
XLA Modules:
  0.0 162.3 jit_solution(17860663842983170609)
XLA Ops:
  0.6 3.8 %collective-permute-start.2 = (bf16[256,128]{1,0:T(8,128)(2,1)}, bf16[256,128]{1,0:T(8,128)(2,1)S(1)}, u32[]{:S(2)}, u32[]{:S(2)}) collective-permute-start(bf16[256,128]{1,0:T(8,128)(2,1)} %param.6), channel_id=1, source_target_pairs={{0,16},{4,20},{8,24},{12,28},{16,0},{20,4},{24,8},{28,12},{32,48},... | collective-permute-start | bytes 196616 | tf_op jit(solution)/shard_map/ppermute | solution.py:141
  4.5 13.5 %collective-permute-start.3 = (bf16[256,128]{1,0:T(8,128)(2,1)}, bf16[256,128]{1,0:T(8,128)(2,1)S(1)}, u32[]{:S(2)}, u32[]{:S(2)}) collective-permute-start(bf16[256,128]{1,0:T(8,128)(2,1)} %param.6), channel_id=1, source_target_pairs={{0,496},{4,500},{8,504},{12,508},{16,32},{20,36},{24,40},{28,44},{... | collective-permute-start | bytes 196616 | tf_op jit(solution)/shard_map/ppermute | solution.py:140
  18.0 9.1 %collective-permute-start.1 = (bf16[512,128]{1,0:T(8,128)(2,1)}, bf16[512,128]{1,0:T(8,128)(2,1)S(1)}, u32[]{:S(2)}, u32[]{:S(2)}) collective-permute-start(bf16[512,128]{1,0:T(8,128)(2,1)} %bitcast.83), channel_id=1, source_target_pairs={{0,2},{1,3},{2,0},{3,1},{4,6},{5,7},{6,4},{7,5},{8,10},{9,11},{10,... | collective-permute-start | bytes 393224 | tf_op jit(solution)/shard_map/ppermute | solution.py:143
  28.2 3.6 %collective-permute-start.4 = (bf16[2,256,128]{2,1,0:T(8,128)(2,1)S(1)}, bf16[2,256,128]{2,1,0:T(8,128)(2,1)S(1)}, u32[]{:S(2)}, u32[]{:S(2)}) collective-permute-start(bf16[2,256,128]{2,1,0:T(8,128)(2,1)S(1)} %get-tuple-element.42), channel_id=1, source_target_pairs={{0,4},{4,8},{8,12},{12,0},{16,20},{20,24},{24,28},{28,16},{32,36},... | collective-permute-start | bytes 393224 | tf_op jit(solution)/shard_map/ppermute | solution.py:151
  31.8 2.8 %collective-permute-start.5 = (bf16[2,256,128]{2,1,0:T(8,128)(2,1)S(1)}, bf16[2,256,128]{2,1,0:T(8,128)(2,1)S(1)}, u32[]{:S(2)}, u32[]{:S(2)}) collective-permute-start(bf16[2,256,128]{2,1,0:T(8,128)(2,1)S(1)} %get-tuple-element.41), channel_id=1, source_target_pairs={{0,8},{4,12},{8,0},{12,4},{16,24},{20,28},{24,16},{28,20},{32,40},... | collective-permute-start | bytes 393224 | tf_op jit(solution)/shard_map/ppermute | solution.py:151
  34.7 4.3 %collective-permute-start.6 = (bf16[2,256,128]{2,1,0:T(8,128)(2,1)S(1)}, bf16[2,256,128]{2,1,0:T(8,128)(2,1)S(1)}, u32[]{:S(2)}, u32[]{:S(2)}) collective-permute-start(bf16[2,256,128]{2,1,0:T(8,128)(2,1)S(1)} %get-tuple-element.40), channel_id=1, source_target_pairs={{0,12},{4,0},{8,4},{12,8},{16,28},{20,16},{24,20},{28,24},{32,44},... | collective-permute-start | bytes 393224 | tf_op jit(solution)/shard_map/ppermute | solution.py:151
  39.0 2.2 %collective-permute-done.1.cross = bf16[512,128]{1,0:T(8,128)(2,1)S(1)} collective-permute-done((bf16[512,128]{1,0:T(8,128)(2,1)}, bf16[512,128]{1,0:T(8,128)(2,1)S(1)}, u32[]{:S(2)}, u32[]{:S(2)}) %collective-permute-start.1) | collective-permute-done | bytes 131104 | tf_op jit(solution)/shard_map/ppermute | solution.py:143
  42.9 1.9 %collective-permute-start.7 = (bf16[1024,128]{1,0:T(8,128)(2,1)S(1)}, bf16[1024,128]{1,0:T(8,128)(2,1)S(1)}, u32[]{:S(2)}, u32[]{:S(2)}) collective-permute-start(bf16[1024,128]{1,0:T(8,128)(2,1)S(1)} %pad_maximum_fusion.1), channel_id=1, source_target_pairs={{0,1},{1,0},{2,3},{3,2},{4,5},{5,4},{6,7},{7,6},{8,9},{9,8},{10,11... | collective-permute-start | bytes 786440 | tf_op jit(solution)/shard_map/ppermute | solution.py:153
  44.9 7.1 %collective-permute-start = (bf16[768,128]{1,0:T(8,128)(2,1)S(1)}, bf16[768,128]{1,0:T(8,128)(2,1)S(1)}, u32[]{:S(2)}, u32[]{:S(2)}) collective-permute-start(bf16[768,128]{1,0:T(8,128)(2,1)S(1)} %constant_dynamic-update-slice_fusion.own), channel_id=1, source_target_pairs={{0,2},{1,3},{2,0},{3,1},{4,6},{5,7},{6,4},{7,5},{8,10},{9,11},{10,... | collective-permute-start | bytes 589832 | tf_op jit(solution)/shard_map/ppermute | solution.py:145
  53.3 2.3 %shard_map.85 = bf16[256,128]{1,0:T(8,128)(2,1)} custom-call(s32[2]{0:T(128)} %pad_add_fusion.ids, s32[2,8]{1,0:T(2,128)} %columns.3, s32[2]{0:T(128)} %counts.3, bf16[512,128]{1,0:T(8,128)(2,1)} %bitcast.84, bf16[512,128]{1,0:T(8,128)(2,1)} %copy-done.1, bf16[1024,128]{1,0:T(8,128)(2,1)} %copy-done.2, bf16[2,128,128]{2,1,0:T(8,128)(2,1)} %bitcast.91, ...), custom_call_target="tpu_custom_call" | custom-call | tf_op jit(solution)/shard_map/pallas_call | solution.py:119
  55.5 14.3 %collective-permute-done.cross = bf16[768,128]{1,0:T(8,128)(2,1)S(1)} collective-permute-done((bf16[768,128]{1,0:T(8,128)(2,1)S(1)}, bf16[768,128]{1,0:T(8,128)(2,1)S(1)}, u32[]{:S(2)}, u32[]{:S(2)}) %collective-permute-start) | collective-permute-done | bytes 196640 | tf_op jit(solution)/shard_map/ppermute | solution.py:145
  70.5 1.9 %collective-permute-start.8 = (bf16[1536,128]{1,0:T(8,128)(2,1)S(1)}, bf16[1536,128]{1,0:T(8,128)(2,1)S(1)}, u32[]{:S(2)}, u32[]{:S(2)}) collective-permute-start(bf16[1536,128]{1,0:T(8,128)(2,1)S(1)} %pad_maximum_fusion), channel_id=1, source_target_pairs={{0,1},{1,0},{2,3},{3,2},{4,5},{5,4},{6,7},{7,6},{8,9},{9,8},{10,11... | collective-permute-start | bytes 1179656 | tf_op jit(solution)/shard_map/ppermute | solution.py:162
  72.4 15.1 %all-gather = bf16[1024,128]{1,0:T(8,128)(2,1)} all-gather(bf16[256,128]{1,0:T(8,128)(2,1)S(1)} %copy-done.10), channel_id=2, replica_groups=mesh['rows'=128,'feat'=4] {'feat'}, dimensions={0}, use_global_device_ids=true | all-gather | bytes 327680 | tf_op jit(solution)/shard_map/all_gather | solution.py:163
  88.3 2.8 %shard_map.86 = (bf16[256,128]{1,0:T(8,128)(2,1)}, bf16[512,128]{1,0:T(8,128)(2,1)}, bf16[256,128]{1,0:T(8,128)(2,1)}) custom-call(s32[2]{0:T(128)} %pad_add_fusion.ids, bf16[768,128]{1,0:T(8,128)(2,1)} %copy-done.8, bf16[768,128]{1,0:T(8,128)(2,1)} %copy-done.3, bf16[1536,128]{1,0:T(8,128)(2,1)} %copy-done.7, bf16[4,256,128]{2,1,0:T(8,128)(2,1)} %bitcast.87), custom_call_target="tpu_custom_call" | custom-call | tf_op jit(solution)/shard_map/pallas_call | solution.py:119
  91.1 16.1 %all-to-all-start = ((bf16[128,4,128]{2,1,0:T(4,128)(2,1)}), bf16[128,4,128]{2,1,0:T(4,128)(2,1)S(1)}, u32[]{:S(2)}, u32[]{:S(2)}) async-start(bf16[128,4,128]{2,1,0:T(4,128)(2,1)} %bitcast.96), calls=%async_computation | async-start | bytes 262144 | tf_op jit(solution)/shard_map/all_to_all | solution.py:175
  107.2 2.5 %shard_map.87 = (f32[6,128,128]{2,1,0:T(8,128)}, bf16[4,128,128]{2,1,0:T(8,128)(2,1)}, bf16[4,128,128]{2,1,0:T(8,128)(2,1)}, bf16[4,128,128]{2,1,0:T(8,128)(2,1)}) custom-call(s32[2]{0:T(128)} %pad_add_fusion.ids, s32[2,8]{1,0:T(2,128)} %columns.3, s32[2]{0:T(128)} %counts.3, bf16[512,128]{1,0:T(8,128)(2,1)} %bitcast.85, bf16[512,128]{1,0:T(8,128)(2,1)} %copy-done.1, ...), custom_call_target="tpu_custom_call" | custom-call | tf_op jit(solution)/shard_map/pallas_call | solution.py:119
  109.6 3.4 %collective-permute-start.9 = (bf16[2,256,128]{2,1,0:T(8,128)(2,1)}, bf16[2,256,128]{2,1,0:T(8,128)(2,1)S(1)}, u32[]{:S(2)}, u32[]{:S(2)}) collective-permute-start(bf16[2,256,128]{2,1,0:T(8,128)(2,1)} %bitcast.99), channel_id=1, source_target_pairs={{0,4},{4,8},{8,12},{12,0},{16,20},{20,24},{24,28},{28,16},{32,36},... | collective-permute-start | bytes 393224 | tf_op jit(solution)/shard_map/ppermute | solution.py:190
  113.0 3.4 %collective-permute-start.10 = (bf16[2,256,128]{2,1,0:T(8,128)(2,1)}, bf16[2,256,128]{2,1,0:T(8,128)(2,1)S(1)}, u32[]{:S(2)}, u32[]{:S(2)}) collective-permute-start(bf16[2,256,128]{2,1,0:T(8,128)(2,1)} %bitcast.98), channel_id=1, source_target_pairs={{0,8},{4,12},{8,0},{12,4},{16,24},{20,28},{24,16},{28,20},{32,40},... | collective-permute-start | bytes 393224 | tf_op jit(solution)/shard_map/ppermute | solution.py:190
  116.4 3.6 %collective-permute-start.11 = (bf16[2,256,128]{2,1,0:T(8,128)(2,1)}, bf16[2,256,128]{2,1,0:T(8,128)(2,1)S(1)}, u32[]{:S(2)}, u32[]{:S(2)}) collective-permute-start(bf16[2,256,128]{2,1,0:T(8,128)(2,1)} %bitcast.97), channel_id=1, source_target_pairs={{0,12},{4,0},{8,4},{12,8},{16,28},{20,16},{24,20},{28,24},{32,44},... | collective-permute-start | bytes 393224 | tf_op jit(solution)/shard_map/ppermute | solution.py:190
  121.2 1.8 %collective-permute-done.10 = bf16[2,256,128]{2,1,0:T(8,128)(2,1)S(1)} collective-permute-done((bf16[2,256,128]{2,1,0:T(8,128)(2,1)}, bf16[2,256,128]{2,1,0:T(8,128)(2,1)S(1)}, u32[]{:S(2)}, u32[]{:S(2)}) %collective-permute-start.10) | collective-permute-done | bytes 131104 | tf_op jit(solution)/shard_map/ppermute | solution.py:190
  125.7 16.2 %all-to-all-start.1 = ((bf16[128,4,128]{2,1,0:T(4,128)(2,1)}), bf16[128,4,128]{2,1,0:T(4,128)(2,1)S(1)}, u32[]{:S(2)}, u32[]{:S(2)}) async-start(bf16[128,4,128]{2,1,0:T(4,128)(2,1)} %broadcast_in_dim.16), calls=%async_computation.1 | async-start | bytes 262144 | tf_op jit(solution)/shard_map/all_to_all | solution.py:202
  142.0 12.8 %collective-permute-start.13 = (bf16[256,128]{1,0:T(8,128)(2,1)S(1)}, bf16[256,128]{1,0:T(8,128)(2,1)S(1)}, u32[]{:S(2)}, u32[]{:S(2)}) collective-permute-start(bf16[256,128]{1,0:T(8,128)(2,1)S(1)} %broadcast_select_fusion), channel_id=1, source_target_pairs={{0,496},{4,500},{8,504},{12,508},{16,32},{20,36},{24,40},{28,44},{... | collective-permute-start | bytes 196616 | tf_op jit(solution)/shard_map/ppermute | solution.py:197
  154.8 1.9 %collective-permute-start.12 = (bf16[256,128]{1,0:T(8,128)(2,1)S(1)}, bf16[256,128]{1,0:T(8,128)(2,1)S(1)}, u32[]{:S(2)}, u32[]{:S(2)}) collective-permute-start(bf16[256,128]{1,0:T(8,128)(2,1)S(1)} %get-tuple-element.29), channel_id=1, source_target_pairs={{0,16},{4,20},{8,24},{12,28},{16,0},{20,4},{24,8},{28,12},{32,48},... | collective-permute-start | bytes 196616 | tf_op jit(solution)/shard_map/ppermute | solution.py:198
  157.3 3.6 %collective-permute-done.12 = bf16[256,128]{1,0:T(8,128)(2,1)S(1)} collective-permute-done((bf16[256,128]{1,0:T(8,128)(2,1)S(1)}, bf16[256,128]{1,0:T(8,128)(2,1)S(1)}, u32[]{:S(2)}, u32[]{:S(2)}) %collective-permute-start.12) | collective-permute-done | bytes 65568 | tf_op jit(solution)/shard_map/ppermute | solution.py:198
  (61 shorter events, 11.1 us)
Async XLA Ops:
  0.6 26.5 %collective-permute-start.2 = (bf16[256,128]{1,0:T(8,128)(2,1)}, bf16[256,128]{1,0:T(8,128)(2,1)S(1)}, u32[]{:S(2)}, u32[]{:S(2)}) collective-permute-start(bf16[256,128]{1,0:T(8,128)(2,1)} %param.6), channel_id=1, source_target_pairs={{0,16},{4,20},{8,24},{12,28},{16,0},{20,4},{24,8},{28,12},{32,48},... | collective-permute-start | bytes 196616 | tf_op jit(solution)/shard_map/ppermute | solution.py:141
  4.5 22.7 %collective-permute-start.3 = (bf16[256,128]{1,0:T(8,128)(2,1)}, bf16[256,128]{1,0:T(8,128)(2,1)S(1)}, u32[]{:S(2)}, u32[]{:S(2)}) collective-permute-start(bf16[256,128]{1,0:T(8,128)(2,1)} %param.6), channel_id=1, source_target_pairs={{0,496},{4,500},{8,504},{12,508},{16,32},{20,36},{24,40},{28,44},{... | collective-permute-start | bytes 196616 | tf_op jit(solution)/shard_map/ppermute | solution.py:140
  18.0 23.2 %collective-permute-start.1 = (bf16[512,128]{1,0:T(8,128)(2,1)}, bf16[512,128]{1,0:T(8,128)(2,1)S(1)}, u32[]{:S(2)}, u32[]{:S(2)}) collective-permute-start(bf16[512,128]{1,0:T(8,128)(2,1)} %bitcast.83), channel_id=1, source_target_pairs={{0,2},{1,3},{2,0},{3,1},{4,6},{5,7},{6,4},{7,5},{8,10},{9,11},{10,... | collective-permute-start | bytes 393224 | tf_op jit(solution)/shard_map/ppermute | solution.py:143
  28.1 10.9 %copy-start.11 = (bf16[256,128]{1,0:T(8,128)(2,1)S(1)}, bf16[256,128]{1,0:T(8,128)(2,1)}, u32[]{:S(2)}) copy-start(bf16[256,128]{1,0:T(8,128)(2,1)} %param.11) | copy-start | bytes 196612
  28.2 14.1 %copy-start = (bf16[2,2,128,128]{3,2,1,0:T(8,128)(2,1)S(1)}, bf16[2,2,128,128]{3,2,1,0:T(8,128)(2,1)}, u32[]{:S(2)}) copy-start(bf16[2,2,128,128]{3,2,1,0:T(8,128)(2,1)} %param.8) | copy-start | bytes 393220
  28.2 13.0 %collective-permute-start.4 = (bf16[2,256,128]{2,1,0:T(8,128)(2,1)S(1)}, bf16[2,256,128]{2,1,0:T(8,128)(2,1)S(1)}, u32[]{:S(2)}, u32[]{:S(2)}) collective-permute-start(bf16[2,256,128]{2,1,0:T(8,128)(2,1)S(1)} %get-tuple-element.42), channel_id=1, source_target_pairs={{0,4},{4,8},{8,12},{12,0},{16,20},{20,24},{24,28},{28,16},{32,36},... | collective-permute-start | bytes 393224 | tf_op jit(solution)/shard_map/ppermute | solution.py:151
  31.8 9.5 %collective-permute-start.5 = (bf16[2,256,128]{2,1,0:T(8,128)(2,1)S(1)}, bf16[2,256,128]{2,1,0:T(8,128)(2,1)S(1)}, u32[]{:S(2)}, u32[]{:S(2)}) collective-permute-start(bf16[2,256,128]{2,1,0:T(8,128)(2,1)S(1)} %get-tuple-element.41), channel_id=1, source_target_pairs={{0,8},{4,12},{8,0},{12,4},{16,24},{20,28},{24,16},{28,20},{32,40},... | collective-permute-start | bytes 393224 | tf_op jit(solution)/shard_map/ppermute | solution.py:151
  34.7 7.6 %collective-permute-start.6 = (bf16[2,256,128]{2,1,0:T(8,128)(2,1)S(1)}, bf16[2,256,128]{2,1,0:T(8,128)(2,1)S(1)}, u32[]{:S(2)}, u32[]{:S(2)}) collective-permute-start(bf16[2,256,128]{2,1,0:T(8,128)(2,1)S(1)} %get-tuple-element.40), channel_id=1, source_target_pairs={{0,12},{4,0},{8,4},{12,8},{16,28},{20,16},{24,20},{28,24},{32,44},... | collective-permute-start | bytes 393224 | tf_op jit(solution)/shard_map/ppermute | solution.py:151
  39.0 5.8 %copy-start.6 = (bf16[512,128]{1,0:T(8,128)(2,1)S(1)}, bf16[512,128]{1,0:T(8,128)(2,1)}, u32[]{:S(2)}) copy-start(bf16[512,128]{1,0:T(8,128)(2,1)} %param.7) | copy-start | bytes 393220
  41.2 1.1 copy-start.1
  41.2 1.1 copy-start.12
  41.3 1.0 copy-start.13
  42.9 9.7 %collective-permute-start.7 = (bf16[1024,128]{1,0:T(8,128)(2,1)S(1)}, bf16[1024,128]{1,0:T(8,128)(2,1)S(1)}, u32[]{:S(2)}, u32[]{:S(2)}) collective-permute-start(bf16[1024,128]{1,0:T(8,128)(2,1)S(1)} %pad_maximum_fusion.1), channel_id=1, source_target_pairs={{0,1},{1,0},{2,3},{3,2},{4,5},{5,4},{6,7},{7,6},{8,9},{9,8},{10,11... | collective-permute-start | bytes 786440 | tf_op jit(solution)/shard_map/ppermute | solution.py:153
  44.8 10.7 %copy-start.8 = (bf16[768,128]{1,0:T(8,128)(2,1)}, bf16[768,128]{1,0:T(8,128)(2,1)S(1)}, u32[]{:S(2)}) copy-start(bf16[768,128]{1,0:T(8,128)(2,1)S(1)} %constant_dynamic-update-slice_fusion.own) | copy-start | bytes 589828
  44.9 24.9 %collective-permute-start = (bf16[768,128]{1,0:T(8,128)(2,1)S(1)}, bf16[768,128]{1,0:T(8,128)(2,1)S(1)}, u32[]{:S(2)}, u32[]{:S(2)}) collective-permute-start(bf16[768,128]{1,0:T(8,128)(2,1)S(1)} %constant_dynamic-update-slice_fusion.own), channel_id=1, source_target_pairs={{0,2},{1,3},{2,0},{3,1},{4,6},{5,7},{6,4},{7,5},{8,10},{9,11},{10,... | collective-permute-start | bytes 589832 | tf_op jit(solution)/shard_map/ppermute | solution.py:145
  55.5 16.9 %copy-start.10 = (bf16[256,128]{1,0:T(8,128)(2,1)S(1)}, bf16[256,128]{1,0:T(8,128)(2,1)}, u32[]{:S(2)}) copy-start(bf16[256,128]{1,0:T(8,128)(2,1)} %shard_map.85) | copy-start | bytes 196612
  70.5 17.1 %collective-permute-start.8 = (bf16[1536,128]{1,0:T(8,128)(2,1)S(1)}, bf16[1536,128]{1,0:T(8,128)(2,1)S(1)}, u32[]{:S(2)}, u32[]{:S(2)}) collective-permute-start(bf16[1536,128]{1,0:T(8,128)(2,1)S(1)} %pad_maximum_fusion), channel_id=1, source_target_pairs={{0,1},{1,0},{2,3},{3,2},{4,5},{5,4},{6,7},{7,6},{8,9},{9,8},{10,11... | collective-permute-start | bytes 1179656 | tf_op jit(solution)/shard_map/ppermute | solution.py:162
  91.1 33.8 %all-to-all-start = ((bf16[128,4,128]{2,1,0:T(4,128)(2,1)}), bf16[128,4,128]{2,1,0:T(4,128)(2,1)S(1)}, u32[]{:S(2)}, u32[]{:S(2)}) async-start(bf16[128,4,128]{2,1,0:T(4,128)(2,1)} %bitcast.96), calls=%async_computation | async-start | bytes 262144 | tf_op jit(solution)/shard_map/all_to_all | solution.py:175
  109.6 11.5 %collective-permute-start.9 = (bf16[2,256,128]{2,1,0:T(8,128)(2,1)}, bf16[2,256,128]{2,1,0:T(8,128)(2,1)S(1)}, u32[]{:S(2)}, u32[]{:S(2)}) collective-permute-start(bf16[2,256,128]{2,1,0:T(8,128)(2,1)} %bitcast.99), channel_id=1, source_target_pairs={{0,4},{4,8},{8,12},{12,0},{16,20},{20,24},{24,28},{28,16},{32,36},... | collective-permute-start | bytes 393224 | tf_op jit(solution)/shard_map/ppermute | solution.py:190
  113.0 10.0 %collective-permute-start.10 = (bf16[2,256,128]{2,1,0:T(8,128)(2,1)}, bf16[2,256,128]{2,1,0:T(8,128)(2,1)S(1)}, u32[]{:S(2)}, u32[]{:S(2)}) collective-permute-start(bf16[2,256,128]{2,1,0:T(8,128)(2,1)} %bitcast.98), channel_id=1, source_target_pairs={{0,8},{4,12},{8,0},{12,4},{16,24},{20,28},{24,16},{28,20},{32,40},... | collective-permute-start | bytes 393224 | tf_op jit(solution)/shard_map/ppermute | solution.py:190
  116.4 8.3 %collective-permute-start.11 = (bf16[2,256,128]{2,1,0:T(8,128)(2,1)}, bf16[2,256,128]{2,1,0:T(8,128)(2,1)S(1)}, u32[]{:S(2)}, u32[]{:S(2)}) collective-permute-start(bf16[2,256,128]{2,1,0:T(8,128)(2,1)} %bitcast.97), channel_id=1, source_target_pairs={{0,12},{4,0},{8,4},{12,8},{16,28},{20,16},{24,20},{28,24},{32,44},... | collective-permute-start | bytes 393224 | tf_op jit(solution)/shard_map/ppermute | solution.py:190
  125.7 35.9 %all-to-all-start.1 = ((bf16[128,4,128]{2,1,0:T(4,128)(2,1)}), bf16[128,4,128]{2,1,0:T(4,128)(2,1)S(1)}, u32[]{:S(2)}, u32[]{:S(2)}) async-start(bf16[128,4,128]{2,1,0:T(4,128)(2,1)} %broadcast_in_dim.16), calls=%async_computation.1 | async-start | bytes 262144 | tf_op jit(solution)/shard_map/all_to_all | solution.py:202
  142.0 15.4 %collective-permute-start.13 = (bf16[256,128]{1,0:T(8,128)(2,1)S(1)}, bf16[256,128]{1,0:T(8,128)(2,1)S(1)}, u32[]{:S(2)}, u32[]{:S(2)}) collective-permute-start(bf16[256,128]{1,0:T(8,128)(2,1)S(1)} %broadcast_select_fusion), channel_id=1, source_target_pairs={{0,496},{4,500},{8,504},{12,508},{16,32},{20,36},{24,40},{28,44},{... | collective-permute-start | bytes 196616 | tf_op jit(solution)/shard_map/ppermute | solution.py:197
  154.8 6.2 %collective-permute-start.12 = (bf16[256,128]{1,0:T(8,128)(2,1)S(1)}, bf16[256,128]{1,0:T(8,128)(2,1)S(1)}, u32[]{:S(2)}, u32[]{:S(2)}) collective-permute-start(bf16[256,128]{1,0:T(8,128)(2,1)S(1)} %get-tuple-element.29), channel_id=1, source_target_pairs={{0,16},{4,20},{8,24},{12,28},{16,0},{20,4},{24,8},{28,12},{32,48},... | collective-permute-start | bytes 196616 | tf_op jit(solution)/shard_map/ppermute | solution.py:198
  (7 other events, 4.9 us)
where the time goes:
time: 163 us; the launch traced here: 162 us
  starting transfers between devices  106 us (65%)
  waiting for transfers between devices  25.2 us (15%)
  blocking collectives  15.1 us (9%)
  Pallas kernels  7.49 us (5%)
  local copies, waits for them, and re-layouts  5.35 us (3%)
  other arithmetic  2.41 us (1%)
    all_to_all x1, starting transfers between devices, on_device(): lax.all_to_all(jnp.broadcast_to(total[None], (R, 4, FB)), 'rows', 0, 0, t...  16.2 us
    all_to_all x1, starting transfers between devices, on_device(): parts = lax.all_to_all(terms.reshape(R, 4, FB), 'rows', 0, 0, tiled=True)  16.1 us
    all_gather x1, blocking collectives, on_device(): agg_full = lax.all_gather(agg, 'feat', axis=0, tiled=False)  15.1 us
    ppermute x1, waiting for transfers between devices, on_device(): cross_w = lax.ppermute(own_w, 'feat', CROSS)  14.3 us
    ppermute x1, starting transfers between devices, on_device(): from_b = lax.ppermute(features, 'rows', SWAP_B)  13.5 us
    ppermute x1, starting transfers between devices, on_device(): back_b = lax.ppermute(jnp.where(even, to_prv, to_nxt), 'rows', SWAP_B)  12.8 us
    ppermute x3, starting transfers between devices, on_device(): lax.ppermute(jnp.stack([features, extra]), 'rows', STEP_Y[k])  10.8 us
    ppermute x3, starting transfers between devices, on_device(): lax.ppermute(sends[k - 1].reshape(2, rows, FB), 'rows', STEP_Y[k])  10.4 us
  transfers between devices with their start and end apart: 16, of which 8 were waited for; matrix products, arithmetic and copies ran while one was open for 2% of the time, Pallas kernels for 3%

commit v1 on v0

--- a/solution.py
+++ b/solution.py
@@ -12,6 +12,8 @@
 RB = 2
 REACH = 4
 STEP_Y = [[(r, r // 4 * 4 + (r + k) % 4) for r in range(R)] for k in range(4)]
+GZ = [[x * 32 + z * 4 + y for z in range(ZL)] for x in range(X) for y in range(Y)]
+GXY = [[x * 32 + z * 4 + y for x in range(X) for y in range(Y)] for z in range(ZL)]
 SWAP_A = [(r, (r + 4) % R if (r // 4) % 2 == 0 else (r - 4) % R) for r in range(R)]
 SWAP_B = [(r, (r - 4) % R if (r // 4) % 2 == 0 else (r + 4) % R) for r in range(R)]
 CROSS = [(f, f ^ 2) for f in range(4)]
@@ -122,7 +124,7 @@
         in_specs=[smem] * len(scalars) + [vmem] * len(args),
         out_specs=jax.tree.map(lambda _: vmem, out_shape),
         scratch_shapes=scratch,
-    )(*scalars, *args)
+    )(*scalars, *(pltpu.with_memory_space_constraint(value, pltpu.VMEM) for value in args))
 
 
 def blocks(value):
@@ -172,7 +174,9 @@
         (ids,),
         own_w, cross_w, pair_w, agg_full,
     )
-    parts = lax.all_to_all(terms.reshape(R, 4, FB), "rows", 0, 0, tiled=True)
+    parts = lax.all_to_all(
+        terms.reshape(16, 32, FB), "rows", 0, 0, axis_index_groups=GXY, tiled=True
+    )
     mine, *sends = call(
         spread_kernel,
         (
@@ -188,6 +192,8 @@
     got = []
     for k in range(1, 4):
         got.append(lax.ppermute(sends[k - 1].reshape(2, rows, FB), "rows", STEP_Y[k]).astype(F32))
+    part = parts.astype(F32).sum(0)
+    layers = lax.all_to_all(jnp.broadcast_to(part[None], (8, 32, FB)), "rows", 0, 0, axis_index_groups=GZ, tiled=True)
     here, to_prv, to_nxt = mine.reshape(3, rows, FB)
     for k in range(1, 4):
         here = here + got[k - 1][0]
@@ -198,9 +204,9 @@
     back_a = lax.ppermute(jnp.where(even, to_nxt, to_prv), "rows", SWAP_A)
     grad_features = (here + back_a.astype(F32) + back_b.astype(F32)).astype(BF16)
 
-    total = (parts.astype(F32).sum(0) * float(rows * R) ** (-0.5)).astype(BF16)
+    total = (layers.sum(0) * float(rows * R) ** (-0.5)).astype(BF16)
     grad_weight = lax.all_to_all(
-        jnp.broadcast_to(total[None], (R, 4, FB)), "rows", 0, 0, tiled=True
+        jnp.broadcast_to(total[None], (16, 32, FB)), "rows", 0, 0, axis_index_groups=GXY, tiled=True
     )
     return hidden, grad_features, grad_weight.reshape(4 * FB, FB).astype(F32)
 
@@ -215,6 +221,4 @@
         P("rows", "feat"),
     )
     out_specs = (P("rows", "feat"), P("rows", "feat"), P(None, "feat"))
-    return jax.shard_map(
-        on_device, mesh=mesh, in_specs=in_specs, out_specs=out_specs, check_vma=False
-    )
+    return jax.shard_map(on_device, mesh=mesh, in_specs=in_specs, out_specs=out_specs, check_vma=False)

time: 163 us -> 152 us (0.933)
  the two profiles are of different devices: /device:TPU:8 before, /device:TPU:32 now
where the time goes in v1:
time: 152 us; the launch traced here: 151 us
  starting transfers between devices  88.5 us (58%)
  waiting for transfers between devices  34.8 us (23%)
  blocking collectives  14.7 us (10%)
  Pallas kernels  5.86 us (4%)
  local copies, waits for them, and re-layouts  4.09 us (3%)
  other arithmetic  2.28 us (1%)
    ppermute x1, waiting for transfers between devices, on_device(): cross_w = lax.ppermute(own_w, 'feat', CROSS)  17.3 us
    all_gather x1, blocking collectives, on_device(): agg_full = lax.all_gather(agg, 'feat', axis=0, tiled=False)  14.7 us
    all_to_all x1, starting transfers between devices, on_device(): lax.all_to_all(jnp.broadcast_to(part[None], (8, 32, FB)), 'rows', 0, 0, a...  12.8 us
    ppermute x3, starting transfers between devices, on_device(): lax.ppermute(jnp.stack([features, extra]), 'rows', STEP_Y[k])  11.7 us
    ppermute x1, starting transfers between devices, on_device(): cross_p = lax.ppermute(own_p, 'feat', CROSS)  11.4 us
    ppermute x3, starting transfers between devices, on_device(): lax.ppermute(sends[k - 1].reshape(2, rows, FB), 'rows', STEP_Y[k])  9.75 us
    ppermute x1, starting transfers between devices, on_device(): back_a = lax.ppermute(jnp.where(even, to_nxt, to_prv), 'rows', SWAP_A)  9.68 us
    ppermute x1, starting transfers between devices, on_device(): from_a = lax.ppermute(features, 'rows', SWAP_A)  7.36 us
  transfers between devices with their start and end apart: 17, of which 5 were waited for; matrix products, arithmetic and copies ran while one was open for 3% of the time, Pallas kernels for 1%

profile of v1, /device:TPU:32, one launch (start us, length us, event | category | flops | bytes accessed | tf_op | source)
XLA Modules:
  0.0 151.2 jit_solution(5529490333346403582)
XLA Ops:
  0.6 7.4 %collective-permute-start.2 = (bf16[256,128]{1,0:T(8,128)(2,1)}, bf16[256,128]{1,0:T(8,128)(2,1)S(1)}, u32[]{:S(2)}, u32[]{:S(2)}) collective-permute-start(bf16[256,128]{1,0:T(8,128)(2,1)} %param.6), channel_id=1, source_target_pairs={{0,16},{4,20},{8,24},{12,28},{16,0},{20,4},{24,8},{28,12},{32,48},... | collective-permute-start | bytes 196616 | tf_op jit(solution)/shard_map/ppermute | solution.py:143
  8.0 1.9 %collective-permute-start.3 = (bf16[256,128]{1,0:T(8,128)(2,1)}, bf16[256,128]{1,0:T(8,128)(2,1)S(1)}, u32[]{:S(2)}, u32[]{:S(2)}) collective-permute-start(bf16[256,128]{1,0:T(8,128)(2,1)} %param.6), channel_id=1, source_target_pairs={{0,496},{4,500},{8,504},{12,508},{16,32},{20,36},{24,40},{28,44},{... | collective-permute-start | bytes 196616 | tf_op jit(solution)/shard_map/ppermute | solution.py:142
  9.9 11.4 %collective-permute-start.1 = (bf16[512,128]{1,0:T(8,128)(2,1)}, bf16[512,128]{1,0:T(8,128)(2,1)S(1)}, u32[]{:S(2)}, u32[]{:S(2)}) collective-permute-start(bf16[512,128]{1,0:T(8,128)(2,1)} %bitcast.84), channel_id=1, source_target_pairs={{0,2},{1,3},{2,0},{3,1},{4,6},{5,7},{6,4},{7,5},{8,10},{9,11},{10,... | collective-permute-start | bytes 393224 | tf_op jit(solution)/shard_map/ppermute | solution.py:145
  22.3 3.6 %collective-permute-start.4 = (bf16[2,256,128]{2,1,0:T(8,128)(2,1)S(1)}, bf16[2,256,128]{2,1,0:T(8,128)(2,1)S(1)}, u32[]{:S(2)}, u32[]{:S(2)}) collective-permute-start(bf16[2,256,128]{2,1,0:T(8,128)(2,1)S(1)} %get-tuple-element.42), channel_id=1, source_target_pairs={{0,4},{4,8},{8,12},{12,0},{16,20},{20,24},{24,28},{28,16},{32,36},... | collective-permute-start | bytes 393224 | tf_op jit(solution)/shard_map/ppermute | solution.py:153
  25.9 4.8 %collective-permute-start.5 = (bf16[2,256,128]{2,1,0:T(8,128)(2,1)S(1)}, bf16[2,256,128]{2,1,0:T(8,128)(2,1)S(1)}, u32[]{:S(2)}, u32[]{:S(2)}) collective-permute-start(bf16[2,256,128]{2,1,0:T(8,128)(2,1)S(1)} %get-tuple-element.41), channel_id=1, source_target_pairs={{0,8},{4,12},{8,0},{12,4},{16,24},{20,28},{24,16},{28,20},{32,40},... | collective-permute-start | bytes 393224 | tf_op jit(solution)/shard_map/ppermute | solution.py:153
  30.7 3.3 %collective-permute-start.6 = (bf16[2,256,128]{2,1,0:T(8,128)(2,1)S(1)}, bf16[2,256,128]{2,1,0:T(8,128)(2,1)S(1)}, u32[]{:S(2)}, u32[]{:S(2)}) collective-permute-start(bf16[2,256,128]{2,1,0:T(8,128)(2,1)S(1)} %get-tuple-element.40), channel_id=1, source_target_pairs={{0,12},{4,0},{8,4},{12,8},{16,28},{20,16},{24,20},{28,24},{32,44},... | collective-permute-start | bytes 393224 | tf_op jit(solution)/shard_map/ppermute | solution.py:153
  34.5 3.0 %collective-permute-done.6 = bf16[2,256,128]{2,1,0:T(8,128)(2,1)S(1)} collective-permute-done((bf16[2,256,128]{2,1,0:T(8,128)(2,1)S(1)}, bf16[2,256,128]{2,1,0:T(8,128)(2,1)S(1)}, u32[]{:S(2)}, u32[]{:S(2)}) %collective-permute-start.6) | collective-permute-done | bytes 131104 | tf_op jit(solution)/shard_map/ppermute | solution.py:153
  37.6 1.9 %collective-permute-start.7 = (bf16[1024,128]{1,0:T(8,128)(2,1)S(1)}, bf16[1024,128]{1,0:T(8,128)(2,1)S(1)}, u32[]{:S(2)}, u32[]{:S(2)}) collective-permute-start(bf16[1024,128]{1,0:T(8,128)(2,1)S(1)} %pad_maximum_fusion.1), channel_id=1, source_target_pairs={{0,1},{1,0},{2,3},{3,2},{4,5},{5,4},{6,7},{7,6},{8,9},{9,8},{10,11... | collective-permute-start | bytes 786440 | tf_op jit(solution)/shard_map/ppermute | solution.py:155
  39.6 7.0 %collective-permute-start = (bf16[768,128]{1,0:T(8,128)(2,1)S(1)}, bf16[768,128]{1,0:T(8,128)(2,1)S(1)}, u32[]{:S(2)}, u32[]{:S(2)}) collective-permute-start(bf16[768,128]{1,0:T(8,128)(2,1)S(1)} %constant_dynamic-update-slice_fusion.own), channel_id=1, source_target_pairs={{0,2},{1,3},{2,0},{3,1},{4,6},{5,7},{6,4},{7,5},{8,10},{9,11},{10,... | collective-permute-start | bytes 589832 | tf_op jit(solution)/shard_map/ppermute | solution.py:147
  48.9 17.3 %collective-permute-done.cross = bf16[768,128]{1,0:T(8,128)(2,1)S(1)} collective-permute-done((bf16[768,128]{1,0:T(8,128)(2,1)S(1)}, bf16[768,128]{1,0:T(8,128)(2,1)S(1)}, u32[]{:S(2)}, u32[]{:S(2)}) %collective-permute-start) | collective-permute-done | bytes 196640 | tf_op jit(solution)/shard_map/ppermute | solution.py:147
  66.2 1.9 %collective-permute-start.8 = (bf16[1536,128]{1,0:T(8,128)(2,1)S(1)}, bf16[1536,128]{1,0:T(8,128)(2,1)S(1)}, u32[]{:S(2)}, u32[]{:S(2)}) collective-permute-start(bf16[1536,128]{1,0:T(8,128)(2,1)S(1)} %pad_maximum_fusion), channel_id=1, source_target_pairs={{0,1},{1,0},{2,3},{3,2},{4,5},{5,4},{6,7},{7,6},{8,9},{9,8},{10,11... | collective-permute-start | bytes 1179656 | tf_op jit(solution)/shard_map/ppermute | solution.py:164
  68.1 14.7 %all-gather = bf16[1024,128]{1,0:T(8,128)(2,1)S(1)} all-gather(bf16[256,128]{1,0:T(8,128)(2,1)S(1)} %copy-done.4), channel_id=2, replica_groups=mesh['rows'=128,'feat'=4] {'feat'}, dimensions={0}, use_global_device_ids=true | all-gather | bytes 327680 | tf_op jit(solution)/shard_map/all_gather | solution.py:165
  82.8 2.1 %shard_map.86 = (bf16[256,128]{1,0:T(8,128)(2,1)}, bf16[512,128]{1,0:T(8,128)(2,1)}, bf16[256,128]{1,0:T(8,128)(2,1)}) custom-call(s32[2]{0:T(128)} %pad_add_fusion.ids, bf16[768,128]{1,0:T(8,128)(2,1)S(1)} %constant_dynamic-update-slice_fusion.own, bf16[768,128]{1,0:T(8,128)(2,1)S(1)} %collective-permute-done.cross, ...), custom_call_target="tpu_custom_call" | custom-call | tf_op jit(solution)/shard_map/pallas_call | solution.py:121
  85.8 2.1 %shard_map.87 = (f32[6,128,128]{2,1,0:T(8,128)}, bf16[4,128,128]{2,1,0:T(8,128)(2,1)}, bf16[4,128,128]{2,1,0:T(8,128)(2,1)}, bf16[4,128,128]{2,1,0:T(8,128)(2,1)}) custom-call(s32[2]{0:T(128)} %pad_add_fusion.ids, s32[2,8]{1,0:T(2,128)} %columns.3, s32[2]{0:T(128)} %counts.3, bf16[512,128]{1,0:T(8,128)(2,1)S(1)} %bitcast.87, ...), custom_call_target="tpu_custom_call" | custom-call | tf_op jit(solution)/shard_map/pallas_call | solution.py:121
  87.9 2.3 %collective-permute-start.9 = (bf16[2,256,128]{2,1,0:T(8,128)(2,1)}, bf16[2,256,128]{2,1,0:T(8,128)(2,1)S(1)}, u32[]{:S(2)}, u32[]{:S(2)}) collective-permute-start(bf16[2,256,128]{2,1,0:T(8,128)(2,1)} %bitcast.98), channel_id=1, source_target_pairs={{0,4},{4,8},{8,12},{12,0},{16,20},{20,24},{24,28},{28,16},{32,36},... | collective-permute-start | bytes 393224 | tf_op jit(solution)/shard_map/ppermute | solution.py:194
  90.1 5.6 %collective-permute-start.10 = (bf16[2,256,128]{2,1,0:T(8,128)(2,1)}, bf16[2,256,128]{2,1,0:T(8,128)(2,1)S(1)}, u32[]{:S(2)}, u32[]{:S(2)}) collective-permute-start(bf16[2,256,128]{2,1,0:T(8,128)(2,1)} %bitcast.97), channel_id=1, source_target_pairs={{0,8},{4,12},{8,0},{12,4},{16,24},{20,28},{24,16},{28,20},{32,40},... | collective-permute-start | bytes 393224 | tf_op jit(solution)/shard_map/ppermute | solution.py:194
  95.7 1.9 %collective-permute-start.11 = (bf16[2,256,128]{2,1,0:T(8,128)(2,1)}, bf16[2,256,128]{2,1,0:T(8,128)(2,1)S(1)}, u32[]{:S(2)}, u32[]{:S(2)}) collective-permute-start(bf16[2,256,128]{2,1,0:T(8,128)(2,1)} %bitcast.96), channel_id=1, source_target_pairs={{0,12},{4,0},{8,4},{12,8},{16,28},{20,16},{24,20},{28,24},{32,44},... | collective-permute-start | bytes 393224 | tf_op jit(solution)/shard_map/ppermute | solution.py:194
  97.7 6.0 %all-to-all-start = ((bf16[16,32,128]{2,1,0:T(8,128)(2,1)}), bf16[16,32,128]{2,1,0:T(8,128)(2,1)S(1)}, u32[]{:S(2)}, u32[]{:S(2)}) async-start(bf16[16,32,128]{2,1,0:T(8,128)(2,1)} %bitcast.29), calls=%async_computation | async-start | bytes 262144 | tf_op jit(solution)/shard_map/all_to_all | solution.py:177
  104.7 6.8 %all-to-all-done = bf16[16,32,128]{2,1,0:T(8,128)(2,1)S(1)} async-done(((bf16[16,32,128]{2,1,0:T(8,128)(2,1)}), bf16[16,32,128]{2,1,0:T(8,128)(2,1)S(1)}, u32[]{:S(2)}, u32[]{:S(2)}) %all-to-all-start) | async-done | bytes 131104 | tf_op jit(solution)/shard_map/all_to_all | solution.py:177
  112.2 12.8 %all-to-all-start.1 = ((f32[8,32,128]{2,1,0:T(8,128)}), f32[8,32,128]{2,1,0:T(8,128)S(1)}, u32[]{:S(2)}, u32[]{:S(2)}) async-start(f32[8,32,128]{2,1,0:T(8,128)} %broadcast_in_dim.22), calls=%async_computation.1 | async-start | bytes 262144 | tf_op jit(solution)/shard_map/all_to_all | solution.py:196
  125.1 3.4 %collective-permute-start.13 = (bf16[256,128]{1,0:T(8,128)(2,1)S(1)}, bf16[256,128]{1,0:T(8,128)(2,1)S(1)}, u32[]{:S(2)}, u32[]{:S(2)}) collective-permute-start(bf16[256,128]{1,0:T(8,128)(2,1)S(1)} %broadcast_select_fusion), channel_id=1, source_target_pairs={{0,496},{4,500},{8,504},{12,508},{16,32},{20,36},{24,40},{28,44},{... | collective-permute-start | bytes 196616 | tf_op jit(solution)/shard_map/ppermute | solution.py:203
  128.5 9.7 %collective-permute-start.12 = (bf16[256,128]{1,0:T(8,128)(2,1)S(1)}, bf16[256,128]{1,0:T(8,128)(2,1)S(1)}, u32[]{:S(2)}, u32[]{:S(2)}) collective-permute-start(bf16[256,128]{1,0:T(8,128)(2,1)S(1)} %get-tuple-element.29), channel_id=1, source_target_pairs={{0,16},{4,20},{8,24},{12,28},{16,0},{20,4},{24,8},{28,12},{32,48},... | collective-permute-start | bytes 196616 | tf_op jit(solution)/shard_map/ppermute | solution.py:204
  138.9 3.7 %all-to-all-start.2 = ((bf16[16,32,128]{2,1,0:T(8,128)(2,1)}), bf16[16,32,128]{2,1,0:T(8,128)(2,1)S(1)}, u32[]{:S(2)}, u32[]{:S(2)}) async-start(bf16[16,32,128]{2,1,0:T(8,128)(2,1)} %broadcast_in_dim.23), calls=%async_computation.2 | async-start | bytes 262144 | tf_op jit(solution)/shard_map/all_to_all | solution.py:208
  143.4 7.1 %all-to-all-done.2 = bf16[16,32,128]{2,1,0:T(8,128)(2,1)S(1)} async-done(((bf16[16,32,128]{2,1,0:T(8,128)(2,1)}), bf16[16,32,128]{2,1,0:T(8,128)(2,1)S(1)}, u32[]{:S(2)}, u32[]{:S(2)}) %all-to-all-start.2) | async-done | bytes 131104 | tf_op jit(solution)/shard_map/all_to_all | solution.py:208
  (47 shorter events, 8.6 us)
Async XLA Ops:
  0.6 20.7 %collective-permute-start.2 = (bf16[256,128]{1,0:T(8,128)(2,1)}, bf16[256,128]{1,0:T(8,128)(2,1)S(1)}, u32[]{:S(2)}, u32[]{:S(2)}) collective-permute-start(bf16[256,128]{1,0:T(8,128)(2,1)} %param.6), channel_id=1, source_target_pairs={{0,16},{4,20},{8,24},{12,28},{16,0},{20,4},{24,8},{28,12},{32,48},... | collective-permute-start | bytes 196616 | tf_op jit(solution)/shard_map/ppermute | solution.py:143
  8.0 13.4 %collective-permute-start.3 = (bf16[256,128]{1,0:T(8,128)(2,1)}, bf16[256,128]{1,0:T(8,128)(2,1)S(1)}, u32[]{:S(2)}, u32[]{:S(2)}) collective-permute-start(bf16[256,128]{1,0:T(8,128)(2,1)} %param.6), channel_id=1, source_target_pairs={{0,496},{4,500},{8,504},{12,508},{16,32},{20,36},{24,40},{28,44},{... | collective-permute-start | bytes 196616 | tf_op jit(solution)/shard_map/ppermute | solution.py:142
  9.9 24.1 %collective-permute-start.1 = (bf16[512,128]{1,0:T(8,128)(2,1)}, bf16[512,128]{1,0:T(8,128)(2,1)S(1)}, u32[]{:S(2)}, u32[]{:S(2)}) collective-permute-start(bf16[512,128]{1,0:T(8,128)(2,1)} %bitcast.84), channel_id=1, source_target_pairs={{0,2},{1,3},{2,0},{3,1},{4,6},{5,7},{6,4},{7,5},{8,10},{9,11},{10,... | collective-permute-start | bytes 393224 | tf_op jit(solution)/shard_map/ppermute | solution.py:145
  21.4 0.8 copy-start.1
  22.2 11.8 %copy-start.5 = (bf16[256,128]{1,0:T(8,128)(2,1)S(1)}, bf16[256,128]{1,0:T(8,128)(2,1)}, u32[]{:S(2)}) copy-start(bf16[256,128]{1,0:T(8,128)(2,1)} %param.11) | copy-start | bytes 196612
  22.3 15.3 %copy-start = (bf16[2,2,128,128]{3,2,1,0:T(8,128)(2,1)S(1)}, bf16[2,2,128,128]{3,2,1,0:T(8,128)(2,1)}, u32[]{:S(2)}) copy-start(bf16[2,2,128,128]{3,2,1,0:T(8,128)(2,1)} %param.8) | copy-start | bytes 393220
  22.3 11.8 %collective-permute-start.4 = (bf16[2,256,128]{2,1,0:T(8,128)(2,1)S(1)}, bf16[2,256,128]{2,1,0:T(8,128)(2,1)S(1)}, u32[]{:S(2)}, u32[]{:S(2)}) collective-permute-start(bf16[2,256,128]{2,1,0:T(8,128)(2,1)S(1)} %get-tuple-element.42), channel_id=1, source_target_pairs={{0,4},{4,8},{8,12},{12,0},{16,20},{20,24},{24,28},{28,16},{32,36},... | collective-permute-start | bytes 393224 | tf_op jit(solution)/shard_map/ppermute | solution.py:153
  25.9 8.6 %collective-permute-start.5 = (bf16[2,256,128]{2,1,0:T(8,128)(2,1)S(1)}, bf16[2,256,128]{2,1,0:T(8,128)(2,1)S(1)}, u32[]{:S(2)}, u32[]{:S(2)}) collective-permute-start(bf16[2,256,128]{2,1,0:T(8,128)(2,1)S(1)} %get-tuple-element.41), channel_id=1, source_target_pairs={{0,8},{4,12},{8,0},{12,4},{16,24},{20,28},{24,16},{28,20},{32,40},... | collective-permute-start | bytes 393224 | tf_op jit(solution)/shard_map/ppermute | solution.py:153
  30.7 6.9 %collective-permute-start.6 = (bf16[2,256,128]{2,1,0:T(8,128)(2,1)S(1)}, bf16[2,256,128]{2,1,0:T(8,128)(2,1)S(1)}, u32[]{:S(2)}, u32[]{:S(2)}) collective-permute-start(bf16[2,256,128]{2,1,0:T(8,128)(2,1)S(1)} %get-tuple-element.40), channel_id=1, source_target_pairs={{0,12},{4,0},{8,4},{12,8},{16,28},{20,16},{24,20},{28,24},{32,44},... | collective-permute-start | bytes 393224 | tf_op jit(solution)/shard_map/ppermute | solution.py:153
  34.0 5.5 %copy-start.3 = (bf16[512,128]{1,0:T(8,128)(2,1)S(1)}, bf16[512,128]{1,0:T(8,128)(2,1)}, u32[]{:S(2)}) copy-start(bf16[512,128]{1,0:T(8,128)(2,1)} %param.7) | copy-start | bytes 393220
  37.6 9.6 %collective-permute-start.7 = (bf16[1024,128]{1,0:T(8,128)(2,1)S(1)}, bf16[1024,128]{1,0:T(8,128)(2,1)S(1)}, u32[]{:S(2)}, u32[]{:S(2)}) collective-permute-start(bf16[1024,128]{1,0:T(8,128)(2,1)S(1)} %pad_maximum_fusion.1), channel_id=1, source_target_pairs={{0,1},{1,0},{2,3},{3,2},{4,5},{5,4},{6,7},{7,6},{8,9},{9,8},{10,11... | collective-permute-start | bytes 786440 | tf_op jit(solution)/shard_map/ppermute | solution.py:155
  39.6 26.6 %collective-permute-start = (bf16[768,128]{1,0:T(8,128)(2,1)S(1)}, bf16[768,128]{1,0:T(8,128)(2,1)S(1)}, u32[]{:S(2)}, u32[]{:S(2)}) collective-permute-start(bf16[768,128]{1,0:T(8,128)(2,1)S(1)} %constant_dynamic-update-slice_fusion.own), channel_id=1, source_target_pairs={{0,2},{1,3},{2,0},{3,1},{4,6},{5,7},{6,4},{7,5},{8,10},{9,11},{10,... | collective-permute-start | bytes 589832 | tf_op jit(solution)/shard_map/ppermute | solution.py:147
  48.9 19.2 %copy-start.4 = (bf16[256,128]{1,0:T(8,128)(2,1)S(1)}, bf16[256,128]{1,0:T(8,128)(2,1)}, u32[]{:S(2)}) copy-start(bf16[256,128]{1,0:T(8,128)(2,1)} %shard_map.85) | copy-start | bytes 196612
  66.2 16.7 %collective-permute-start.8 = (bf16[1536,128]{1,0:T(8,128)(2,1)S(1)}, bf16[1536,128]{1,0:T(8,128)(2,1)S(1)}, u32[]{:S(2)}, u32[]{:S(2)}) collective-permute-start(bf16[1536,128]{1,0:T(8,128)(2,1)S(1)} %pad_maximum_fusion), channel_id=1, source_target_pairs={{0,1},{1,0},{2,3},{3,2},{4,5},{5,4},{6,7},{7,6},{8,9},{9,8},{10,11... | collective-permute-start | bytes 1179656 | tf_op jit(solution)/shard_map/ppermute | solution.py:164
  85.0 0.8 copy-start.2
  87.9 37.1 %collective-permute-start.9 = (bf16[2,256,128]{2,1,0:T(8,128)(2,1)}, bf16[2,256,128]{2,1,0:T(8,128)(2,1)S(1)}, u32[]{:S(2)}, u32[]{:S(2)}) collective-permute-start(bf16[2,256,128]{2,1,0:T(8,128)(2,1)} %bitcast.98), channel_id=1, source_target_pairs={{0,4},{4,8},{8,12},{12,0},{16,20},{20,24},{24,28},{28,16},{32,36},... | collective-permute-start | bytes 393224 | tf_op jit(solution)/shard_map/ppermute | solution.py:194
  90.1 34.8 %collective-permute-start.10 = (bf16[2,256,128]{2,1,0:T(8,128)(2,1)}, bf16[2,256,128]{2,1,0:T(8,128)(2,1)S(1)}, u32[]{:S(2)}, u32[]{:S(2)}) collective-permute-start(bf16[2,256,128]{2,1,0:T(8,128)(2,1)} %bitcast.97), channel_id=1, source_target_pairs={{0,8},{4,12},{8,0},{12,4},{16,24},{20,28},{24,16},{28,20},{32,40},... | collective-permute-start | bytes 393224 | tf_op jit(solution)/shard_map/ppermute | solution.py:194
  95.7 29.3 %collective-permute-start.11 = (bf16[2,256,128]{2,1,0:T(8,128)(2,1)}, bf16[2,256,128]{2,1,0:T(8,128)(2,1)S(1)}, u32[]{:S(2)}, u32[]{:S(2)}) collective-permute-start(bf16[2,256,128]{2,1,0:T(8,128)(2,1)} %bitcast.96), channel_id=1, source_target_pairs={{0,12},{4,0},{8,4},{12,8},{16,28},{20,16},{24,20},{28,24},{32,44},... | collective-permute-start | bytes 393224 | tf_op jit(solution)/shard_map/ppermute | solution.py:194
  97.7 13.8 %all-to-all-start = ((bf16[16,32,128]{2,1,0:T(8,128)(2,1)}), bf16[16,32,128]{2,1,0:T(8,128)(2,1)S(1)}, u32[]{:S(2)}, u32[]{:S(2)}) async-start(bf16[16,32,128]{2,1,0:T(8,128)(2,1)} %bitcast.29), calls=%async_computation | async-start | bytes 262144 | tf_op jit(solution)/shard_map/all_to_all | solution.py:177
  112.2 26.0 %all-to-all-start.1 = ((f32[8,32,128]{2,1,0:T(8,128)}), f32[8,32,128]{2,1,0:T(8,128)S(1)}, u32[]{:S(2)}, u32[]{:S(2)}) async-start(f32[8,32,128]{2,1,0:T(8,128)} %broadcast_in_dim.22), calls=%async_computation.1 | async-start | bytes 262144 | tf_op jit(solution)/shard_map/all_to_all | solution.py:196
  125.1 17.5 %collective-permute-start.13 = (bf16[256,128]{1,0:T(8,128)(2,1)S(1)}, bf16[256,128]{1,0:T(8,128)(2,1)S(1)}, u32[]{:S(2)}, u32[]{:S(2)}) collective-permute-start(bf16[256,128]{1,0:T(8,128)(2,1)S(1)} %broadcast_select_fusion), channel_id=1, source_target_pairs={{0,496},{4,500},{8,504},{12,508},{16,32},{20,36},{24,40},{28,44},{... | collective-permute-start | bytes 196616 | tf_op jit(solution)/shard_map/ppermute | solution.py:203
  128.5 14.1 %collective-permute-start.12 = (bf16[256,128]{1,0:T(8,128)(2,1)S(1)}, bf16[256,128]{1,0:T(8,128)(2,1)S(1)}, u32[]{:S(2)}, u32[]{:S(2)}) collective-permute-start(bf16[256,128]{1,0:T(8,128)(2,1)S(1)} %get-tuple-element.29), channel_id=1, source_target_pairs={{0,16},{4,20},{8,24},{12,28},{16,0},{20,4},{24,8},{28,12},{32,48},... | collective-permute-start | bytes 196616 | tf_op jit(solution)/shard_map/ppermute | solution.py:204
  138.9 11.6 %all-to-all-start.2 = ((bf16[16,32,128]{2,1,0:T(8,128)(2,1)}), bf16[16,32,128]{2,1,0:T(8,128)(2,1)S(1)}, u32[]{:S(2)}, u32[]{:S(2)}) async-start(bf16[16,32,128]{2,1,0:T(8,128)(2,1)} %broadcast_in_dim.23), calls=%async_computation.2 | async-start | bytes 262144 | tf_op jit(solution)/shard_map/all_to_all | solution.py:208
